TPU v7x, 32 devices: a whole 2x2x4 slice. The times are simulated.
32 devices in a mesh: replica: 4 (over y, core), fsdp: 4 (over z), tensor: 2 (over x).
Axes of the slice: x: 2, y: 2, z: 4, core: 2. Of those that a mesh axis runs over, the one named last changes fastest.
Arguments:
- tokens: bfloat16 [8192, 8192], P(('replica', 'fsdp')), may hold values from -6 to 6
- norm_gain: float32 [8192], replicated, may hold values from 0.1 to 1.9
- outer_base: float32 [2, 8192, 1024], P(None, 'fsdp', 'tensor'), may hold values from -0.0625 to 0.0625
- momentum: float32 [2, 8192, 1024], P(None, 'fsdp', 'tensor'), may hold values from -0.06 to 0.06
- inner_params: bfloat16 [4, 2, 8192, 1024], P('replica', None, 'fsdp', 'tensor'), may hold values from -0.0625 to 0.0625
Outputs:
- new_base: float32 [2, 8192, 1024], P(None, ('fsdp', 'replica'), 'tensor')
- new_momentum: float32 [2, 8192, 1024], P(None, ('fsdp', 'replica'), 'tensor')
- keys: bfloat16 [8192, 1024], P(('replica', 'fsdp'), 'tensor')
- values: bfloat16 [8192, 1024], P(('replica', 'fsdp'), 'tensor')
All inputs are finite; a program needn't handle non-finite values.
Results may differ from a plain program's by a relative error of at most 0.018.
Values may be sent and summed in bfloat16 or wider, within the bound.
A program may use at most 128 MiB of HBM per device.

v0:
```python
import jax
import jax.numpy as jnp
from jax import lax
from jax.sharding import PartitionSpec as P

momentum_rate = 0.9
outer_rate = 0.7
epsilon = 1e-05


def normalize(tokens, norm_gain):
    inputs = tokens.astype(jnp.float32)
    scale = lax.rsqrt(jnp.mean(inputs * inputs, axis=-1, keepdims=True) + epsilon)
    return (inputs * scale * norm_gain).astype(jnp.bfloat16)


def nesterov(outer_base, momentum, average):
    new_momentum = momentum_rate * momentum + average
    new_base = outer_base - outer_rate * (average + momentum_rate * new_momentum)
    return (new_base, new_momentum)


def make_share_adder(normed, quarter, groups, replicas):

    def feature_start(position):
        block = position // quarter
        within = position % quarter
        source_replica = block // groups
        source_group = block % groups
        return (source_group * replicas + source_replica) * quarter + within

    def add_block(totals, portion, position):
        columns = lax.dynamic_slice_in_dim(normed, feature_start(position), portion.shape[1], 1)
        first = totals[0] + jnp.dot(columns, portion[0], preferred_element_type=jnp.float32)
        second = totals[1] + jnp.dot(columns, portion[1], preferred_element_type=jnp.float32)
        return (first, second)

    def add_rows(totals, portion, offset):
        length = portion.shape[1]
        blocks = length // quarter

        def one_block(index, carry):
            sliced = lax.dynamic_slice_in_dim(portion, index * quarter, quarter, 1)
            return add_block(carry, sliced, index * quarter)

        return lax.fori_loop(0, blocks, one_block, totals)

    return add_rows


def on_device(tokens, norm_gain, outer_base, momentum, inner_params):
    normed = normalize(tokens, norm_gain)
    deltas = (outer_base - inner_params[0].astype(jnp.float32)).astype(jnp.bfloat16)
    replicas = lax.axis_size("replica")
    shard_rows = outer_base.shape[1]
    quarter = shard_rows // replicas
    replica_index = lax.axis_index("replica")
    row_count = normed.shape[0]
    empty = jnp.zeros((row_count, outer_base.shape[2]), jnp.float32)
    terms = deltas.astype(jnp.float32)
    share = lax.psum_scatter(
        terms.astype(jnp.bfloat16), "replica", scatter_dimension=1, tiled=True
    ).astype(jnp.float32)
    base_part = lax.dynamic_slice_in_dim(outer_base, replica_index * quarter, quarter, 1)
    momentum_part = lax.dynamic_slice_in_dim(momentum, replica_index * quarter, quarter, 1)
    new_base, new_momentum = nesterov(base_part, momentum_part, share / replicas)
    weights = new_base.astype(jnp.bfloat16)
    groups = lax.axis_size("fsdp")
    adder = make_share_adder(normed, quarter, groups, replicas)
    keys, values = adder(
        (empty, empty),
        lax.all_gather(weights, ("replica", "fsdp"), axis=1, tiled=True),
        jnp.int32(0),
    )
    return (new_base, new_momentum, keys.astype(jnp.bfloat16), values.astype(jnp.bfloat16))


def solution(mesh):
    placed = (
        P(("replica", "fsdp"), None),
        P(),
        P(None, "fsdp", "tensor"),
        P(None, "fsdp", "tensor"),
        P("replica", None, "fsdp", "tensor"),
    )
    return jax.shard_map(
        on_device,
        mesh=mesh,
        in_specs=placed,
        out_specs=(
            P(None, ("fsdp", "replica"), "tensor"),
            P(None, ("fsdp", "replica"), "tensor"),
            P(("replica", "fsdp"), "tensor"),
            P(("replica", "fsdp"), "tensor"),
        ),
        check_vma=False,
    )
```

profile of v0, /device:TPU:0, one launch (start us, length us, event | category | flops | bytes accessed | tf_op | source)
XLA Modules:
  0.0 263.4 jit_solution(9171429785954920437)
XLA Ops:
  7.2 8.0 %fusion.7 = bf16[2,2048,512]{2,1,0:T(8,128)(2,1)} fusion(f32[2,2048,512]{2,1,0:T(8,128)} %param.9, bf16[1,2,2048,512]{3,2,1,0:T(8,128)(2,1)} %param.11), kind=kLoop, calls=%fused_computation.14 | loop fusion | flops 6291456 | bytes 16777216 | tf_op jit(solution)/shard_map/convert_element_type | solution.py:53
  15.3 47.4 %reduce-scatter.2.cloned.1.call-done = bf16[2,512,512]{2,1,0:T(8,128)(2,1)} async-done(((bf16[2,2048,512]{2,1,0:T(8,128)(2,1)}), bf16[2,512,512]{2,1,0:T(8,128)(2,1)}) %reduce-scatter.2.cloned.1.call-update) | async-done | bytes 1048592 | tf_op jit(solution)/shard_map/reduce_scatter | solution.py:61
  62.7 5.8 %fusion.8 = (bf16[2,512,512]{2,1,0:T(8,128)(2,1)}, f32[2,512,512]{2,1,0:T(8,128)}, f32[2,512,512]{2,1,0:T(8,128)}) fusion(bf16[2,512,512]{2,1,0:T(8,128)(2,1)} %reduce-scatter.2.cloned.1.call-done, f32[2,2048,512]{2,1,0:T(8,128)} %param.9, s32[]{:T(128)S(6)} %select_n.89, f32[2,2048,512]{2,1,0:T(8,128)} %param.10), kind=kLoop, calls=%fused_computation.19 | loop fusion | flops 4718592 | bytes 10485764 | tf_op jit(solution)/shard_map/convert_element_type | solution.py:67
  68.5 5.1 %fusion.4 = f32[512]{0:T(512)S(1)} fusion(bf16[512,8192]{1,0:T(8,128)(2,1)} %param.7), kind=kLoop, calls=%fused_computation.10 | loop fusion | flops 12582400 | bytes 8390656 | tf_op jit(solution)/shard_map/reduce_sum | solution.py:13
  73.6 10.4 %fusion.6 = bf16[512,8192]{1,0:T(8,128)(2,1)} fusion(bf16[512,8192]{1,0:T(8,128)(2,1)} %param.7, f32[8192]{0:T(1024)S(1)} %copy-done, f32[512]{0:T(512)S(1)} %add_rsqrt_fusion), kind=kLoop, calls=%fused_computation.12 | loop fusion | flops 16777216 | bytes 16812032 | tf_op jit(solution)/shard_map/convert_element_type | solution.py:14
  84.0 111.1 %all-gather.2.cloned.1.call-done = bf16[2,8192,512]{2,1,0:T(8,128)(2,1)} async-done(((bf16[2,512,512]{2,1,0:T(8,128)(2,1)}), bf16[2,8192,512]{2,1,0:T(8,128)(2,1)}) %all-gather.2.cloned.1.call-update) | async-done | bytes 16777232 | tf_op jit(solution)/shard_map/all_gather | solution.py:72
  195.1 59.8 %while.19 = (s32[]{:T(128)}, f32[512,512]{1,0:T(8,128)S(1)}, f32[512,512]{1,0:T(8,128)S(1)}, bf16[512,8192]{1,0:T(8,128)(2,1)}, bf16[2,8192,512]{2,1,0:T(8,128)(...) while((s32[]{:T(128)}, f32[512,512]{1,0:T(8,128)S(1)}, ...), condition=%wide.region_3.4_spmd.clone, body=%wide.region_2.3_spmd.clone.sunk | while | flops 537919552 | bytes 6292149 | solution.py:46
  196.9 1.8 convolution_add_fusion.4
  198.8 1.8 convolution_add_fusion.5
  200.6 1.8 convolution_add_fusion.4
  202.5 1.8 convolution_add_fusion.5
  204.4 1.8 convolution_add_fusion.4
  206.3 1.8 convolution_add_fusion.5
  210.0 1.8 convolution_add_fusion.5
  213.8 1.8 convolution_add_fusion.5
  217.5 1.8 convolution_add_fusion.5
  221.3 1.8 convolution_add_fusion.5
  225.0 1.8 convolution_add_fusion.5
  228.8 1.8 convolution_add_fusion.5
  232.5 1.8 convolution_add_fusion.5
  236.3 1.8 convolution_add_fusion.5
  240.0 1.8 convolution_add_fusion.5
  243.8 1.8 convolution_add_fusion.5
  247.5 1.8 convolution_add_fusion.5
  (26 shorter events, 29.1 us)
Async XLA Ops:
  7.2 55.5 %reduce-scatter.2.cloned.1.call-start = ((), (), s32[]{:S(2)}) async-start(), calls=%async_computation.1 | async-start | bytes 5242880 | tf_op jit(solution)/shard_map/reduce_scatter | solution.py:61
  15.2 179.9 %all-gather.2.cloned.1.call-start = ((), (), s32[]{:S(2)}) async-start(), calls=%async_computation.2 | async-start | bytes 17825792 | tf_op jit(solution)/shard_map/all_gather | solution.py:72
  15.3 58.3 %copy-start = (f32[8192]{0:T(1024)S(1)}, f32[8192]{0:T(1024)}, u32[]{:S(2)}) copy-start(f32[8192]{0:T(1024)} %param.8) | copy-start | bytes 98308
Sparse Core Ops, SparseCore 0:
  15.3 47.2 reduce-scatter.1
  68.6 126.4 all-gather.1
where the time goes:
time: 264 us; the launch traced here: 263 us
  waiting for transfers between devices  158 us (60%)
  matrix products  58.3 us (22%)
  other arithmetic  31 us (12%)
  between operations  14.1 us (5%)
    all_gather x1, waiting for transfers between devices, on_device(): lax.all_gather(weights, ('replica', 'fsdp'), axis=1, tiled=True)  111 us
    reduce_scatter x1, waiting for transfers between devices, on_device(): lax.psum_scatter(terms.astype(jnp.bfloat16), 'replica', scatter_dimension...  47.4 us
    dot_general x16, matrix products, add_block(): jnp.dot(columns, portion[1], preferred_element_type=jnp.float32)  29.2 us
    dot_general x16, matrix products, add_block(): jnp.dot(columns, portion[0], preferred_element_type=jnp.float32)  29.1 us
    convert_element_type x1, other arithmetic, normalize(): return (inputs * scale * norm_gain).astype(jnp.bfloat16)  10.4 us
    convert_element_type x1, other arithmetic, on_device(): (outer_base - inner_params[0].astype(jnp.float32)).astype(jnp.bfloat16)  7.97 us
    convert_element_type x1, other arithmetic, on_device(): weights = new_base.astype(jnp.bfloat16)  5.8 us
  transfers between devices with their start and end apart: 2, of which 2 were waited for; matrix products, arithmetic and copies ran while one was open for 6% of the time, Pallas kernels for 0%

commit v1 on v0

v1 whole, which is shorter than its diff:
```python
import functools

import jax
import jax.numpy as jnp
from jax import lax
from jax.experimental import pallas as pl
from jax.experimental.pallas import tpu as pltpu
from jax.sharding import PartitionSpec as P

momentum_rate = 0.9
outer_rate = 0.7
epsilon = 1e-05
MESH = pl.DeviceIdType.MESH
CHUNKS = 4
FIRST_Z = 3


def kernel(
    depth, tok_h, gain_ref, base_h, mom_h, inner_h,
    nb_h, nm_h, keys_ref, values_ref,
    tok, base, inner, mom, nb, w, ps, pr, ys, yr, acc,
    in_sem, tok_sem, out_sem, ps_sem, pr_sem, ys_sem, yr_sem,
    w_recv, right_sem, left_sem, cross_sem, pair_sem,
):
    r = lax.axis_index("replica")
    z = lax.axis_index("fsdp")
    x = lax.axis_index("tensor")
    y, c = r // 2, r % 2
    oy, oc = 1 - y, 1 - c
    pair = (y * 2 + oc, z, x)
    cross = (oy * 2 + c, z, x)
    right = (r, z + 1, x)
    left = (r, z - 1, x)
    rows = w.shape[-2]
    token_rows = tok.shape[0]

    def load(k):
        m, h = k // 2, k % 2
        return (
            pltpu.make_async_copy(base_h.at[m, :, h], base.at[k], in_sem.at[k, 0]),
            pltpu.make_async_copy(inner_h.at[m, :, h], inner.at[k], in_sem.at[k, 1]),
        )

    def load_momentum(k):
        return pltpu.make_async_copy(mom_h.at[k // 2, r, k % 2], mom.at[k], in_sem.at[k, 2])

    load_tokens = pltpu.make_async_copy(tok_h, tok, tok_sem)
    for k in range(CHUNKS):
        for copy in load(k):
            copy.start()
    load_tokens.start()
    for k in range(CHUNKS):
        load_momentum(k).start()
    acc[...] = jnp.zeros_like(acc)

    barrier = pltpu.get_barrier_semaphore()
    for peer in (pair, cross):
        pl.semaphore_signal(barrier, inc=1, device_id=peer, device_id_type=MESH)

    @pl.when(z < depth - 1)
    def _():
        pl.semaphore_signal(barrier, inc=1, device_id=right, device_id_type=MESH)

    @pl.when(z > 0)
    def _():
        pl.semaphore_signal(barrier, inc=1, device_id=left, device_id_type=MESH)

    neighbours = jnp.where(z < depth - 1, 1, 0) + jnp.where(z > 0, 1, 0)
    pl.semaphore_wait(barrier, 2 + neighbours)

    def delta(k, target):
        return (base[k, target] - inner[k, target].astype(jnp.float32)).astype(jnp.bfloat16)

    def to_pair(k):
        return pltpu.make_async_remote_copy(
            ps.at[k], pr.at[k], ps_sem.at[k], pr_sem.at[k], device_id=pair, device_id_type=MESH)

    def to_cross(k):
        return pltpu.make_async_remote_copy(
            ys.at[k], yr.at[k], ys_sem.at[k], yr_sem.at[k], device_id=cross, device_id_type=MESH)

    for k in range(CHUNKS + 1):
        if k < CHUNKS:
            for copy in load(k):
                copy.wait()
            ps[k, 1] = delta(k, oy * 2 + oc)
            ps[k, 0] = delta(k, y * 2 + oc)
            to_pair(k).start()
        if k > 0:
            j = k - 1
            to_pair(j).wait_recv()
            ys[j] = (delta(j, oy * 2 + c).astype(jnp.float32) + pr[j, 1].astype(jnp.float32)).astype(jnp.bfloat16)
            to_cross(j).start()

    def send(yl, o, k, peer, sem):
        block = w.at[c, yl, o, k]
        return pltpu.make_async_remote_copy(
            block, block, sem, w_recv.at[c, yl, o, k], device_id=peer, device_id_type=MESH)

    def send_right(yl, o, k):
        return send(yl, o, k, right, right_sem.at[yl, o, k])

    def send_left(yl, o, k):
        return send(yl, o, k, left, left_sem.at[yl, o, k])

    def send_cross(yl, o, k):
        return send(yl, o, k, cross, cross_sem.at[o, k])

    def send_pair(yl, o, k):
        return send(yl, o, k, pair, pair_sem.at[yl, o, k])

    def arrived(cc, yl, o, k):
        block = w.at[cc, yl, o, k]
        pltpu.make_async_copy(block, block, w_recv.at[cc, yl, o, k]).wait()

    def along(yl, o, k, do_right, do_left):
        if do_right:
            @pl.when(z < depth - 1)
            def _():
                send_right(yl, o, k).start()
        if do_left:
            @pl.when(z > 0)
            def _():
                send_left(yl, o, k).start()

    def multiply(cc, yl, o, k):
        m, h = k // 2, k % 2
        first = pl.multiple_of(((o * 4 + yl * 2 + cc) * 2 + h) * rows, rows)
        acc[m] += jnp.dot(tok[:, pl.ds(first, rows)], w[cc, yl, o, k], preferred_element_type=jnp.float32)

    def normalize(i):
        at = pl.ds(pl.multiple_of(i * 16, 16), 16)
        value = tok[at, :].astype(jnp.float32)
        scale = lax.rsqrt(jnp.mean(value * value, axis=-1, keepdims=True) + epsilon)
        tok[at, :] = (value * scale * gain_ref[...]).astype(jnp.bfloat16)

    def out_copies(k):
        m, h = k // 2, k % 2
        return (
            pltpu.make_async_copy(nb.at[k], nb_h.at[m, h], out_sem.at[k, 0]),
            pltpu.make_async_copy(mom.at[k], nm_h.at[m, h], out_sem.at[k, 1]),
        )

    load_tokens.wait()
    strips = token_rows // 16
    for k in range(CHUNKS):
        lax.fori_loop(k * strips // CHUNKS, (k + 1) * strips // CHUNKS, lambda i, s: (normalize(i), s)[1], 0)
        load_momentum(k).wait()
        to_cross(k).wait_recv()
        total = (
            delta(k, r).astype(jnp.float32) + pr[k, 0].astype(jnp.float32) + yr[k].astype(jnp.float32))
        average = total / 4
        new_momentum = momentum_rate * mom[k] + average
        new_base = base[k, r] - outer_rate * (average + momentum_rate * new_momentum)
        w[c, y, z, k] = new_base.astype(jnp.bfloat16)
        mom[k] = new_momentum
        nb[k] = new_base
        along(y, z, k, True, True)
        send_cross(y, z, k).start()
        send_pair(y, z, k).start()
        for copy in out_copies(k):
            copy.start()

    def loop(count, body):
        lax.fori_loop(0, count, lambda i, s: (body(i), s)[1], 0)

    def both_sides(g, body):
        @pl.when(z - g >= 0)
        def _():
            body(z - g, True, False)

        @pl.when(z + g < depth)
        def _():
            body(z + g, False, True)

    def multiply_all(g, blocks, place):
        def one(i):
            cc, side, b = (i // 2) % 2, i % 2, i // 4
            o = z + (2 * side - 1) * g
            yl, k = place(b)

            @pl.when((o >= 0) & (o < depth))
            def _():
                @pl.when(cc == 1)
                def _():
                    arrived(oc, yl, o, k)
                multiply((c + cc) % 2, yl, o, k)
        loop(4 * blocks, one)

    def own_products(i):
        k, cc = i // 2, i % 2

        @pl.when(cc == 1)
        def _():
            arrived(oc, y, z, k)
        multiply((c + cc) % 2, y, z, k)

    loop(2 * CHUNKS, own_products)

    late = CHUNKS - FIRST_Z

    def first_stage(g):
        def one(k):
            def relay(o, do_right, do_left):
                arrived(c, y, o, k)
                along(y, o, k, do_right, do_left)
                send_cross(y, o, k).start()
                send_pair(y, o, k).start()
            both_sides(g, relay)
        loop(FIRST_Z, one)

        @pl.when(g == min(2, depth - 1))
        def _():
            for k in range(FIRST_Z, CHUNKS):
                arrived(c, oy, z, k)
                along(oy, z, k, True, True)
                send_pair(oy, z, k).start()

        multiply_all(g, FIRST_Z, lambda b: (y, b))

    lax.fori_loop(1, depth, lambda g, s: (first_stage(g), s)[1], 0)

    def from_cross(k):
        arrived(c, oy, z, k)
        send_pair(oy, z, k).start()

    loop(FIRST_Z, from_cross)

    def cross_products(i):
        k, cc = i // 2, i % 2

        @pl.when(cc == 1)
        def _():
            arrived(oc, oy, z, k)
        multiply((c + cc) % 2, oy, z, k)

    loop(2 * CHUNKS, cross_products)

    def second_stage(g):
        def one(i):
            yl, k = i % 2, FIRST_Z + i // 2

            def relay(o, do_right, do_left):
                arrived(c, yl, o, k)
                along(yl, o, k, do_right, do_left)
                send_pair(yl, o, k).start()
            both_sides(g, relay)
        loop(2 * late, one)
        multiply_all(g, 2 * late, lambda b: (b % 2, FIRST_Z + b // 2))

        def two(k):
            def relay(o, do_right, do_left):
                arrived(c, oy, o, k)
                send_pair(oy, o, k).start()
            both_sides(g, relay)
        loop(FIRST_Z, two)
        multiply_all(g, FIRST_Z, lambda b: (oy, b))

    lax.fori_loop(1, depth, lambda g, s: (second_stage(g), s)[1], 0)

    keys_ref[...] = acc[0].astype(keys_ref.dtype)
    values_ref[...] = acc[1].astype(values_ref.dtype)

    for k in range(CHUNKS):
        to_pair(k).wait_send()
        to_cross(k).wait_send()
        for copy in out_copies(k):
            copy.wait()

    def drain(i):
        o, k = i // CHUNKS, i % CHUNKS

        @pl.when((k < FIRST_Z) | (o == z))
        def _():
            send_cross(y, o, k).wait_send()

        for yl in range(2):
            send_pair(yl, o, k).wait_send()

            @pl.when((k >= FIRST_Z) | (yl == y))
            def _():
                @pl.when((o <= z) & (z < depth - 1))
                def _():
                    send_right(yl, o, k).wait_send()

                @pl.when((o >= z) & (z > 0))
                def _():
                    send_left(yl, o, k).wait_send()

    loop(depth * CHUNKS, drain)


def on_device(tokens, norm_gain, outer_base, momentum, inner_params):
    depth = lax.axis_size("fsdp")
    replicas = lax.axis_size("replica")
    assert replicas == 4
    quarter = outer_base.shape[1] // replicas
    rows, columns = quarter // 2, outer_base.shape[2]
    count, features = tokens.shape
    split = (2, replicas, 2, rows, columns)
    anywhere = pl.BlockSpec(memory_space=pl.ANY)
    vmem = pl.BlockSpec(memory_space=pltpu.VMEM)
    dma = pltpu.SemaphoreType.DMA
    f32, bf16 = jnp.float32, jnp.bfloat16
    piece = (rows, columns)
    new_base, new_momentum, keys, values = pl.pallas_call(
        functools.partial(kernel, depth),
        name="outer_step",
        out_shape=(
            jax.ShapeDtypeStruct((2, 2) + piece, f32),
            jax.ShapeDtypeStruct((2, 2) + piece, f32),
            jax.ShapeDtypeStruct((count, columns), bf16),
            jax.ShapeDtypeStruct((count, columns), bf16),
        ),
        in_specs=[anywhere, vmem, anywhere, anywhere, anywhere],
        out_specs=(anywhere, anywhere, vmem, vmem),
        scratch_shapes=[
            pltpu.VMEM((count, features), bf16),
            pltpu.VMEM((CHUNKS, replicas) + piece, f32),
            pltpu.VMEM((CHUNKS, replicas) + piece, bf16),
            pltpu.VMEM((CHUNKS,) + piece, f32),
            pltpu.VMEM((CHUNKS,) + piece, f32),
            pltpu.VMEM((2, 2, depth, CHUNKS) + piece, bf16),
            pltpu.VMEM((CHUNKS, 2) + piece, bf16),
            pltpu.VMEM((CHUNKS, 2) + piece, bf16),
            pltpu.VMEM((CHUNKS,) + piece, bf16),
            pltpu.VMEM((CHUNKS,) + piece, bf16),
            pltpu.VMEM((2, count, columns), f32),
            dma((CHUNKS, 3)), dma, dma((CHUNKS, 2)),
            dma((CHUNKS,)), dma((CHUNKS,)), dma((CHUNKS,)), dma((CHUNKS,)),
            dma((2, 2, depth, CHUNKS)),
            dma((2, depth, CHUNKS)), dma((2, depth, CHUNKS)), dma((depth, CHUNKS)), dma((2, depth, CHUNKS)),
        ],
        compiler_params=pltpu.CompilerParams(
            collective_id=0, has_side_effects=True, vmem_limit_bytes=60 * 1024 * 1024),
    )(
        tokens,
        norm_gain.reshape(1, features),
        outer_base.reshape(split),
        momentum.reshape(split),
        inner_params.reshape(split),
    )
    share = (2, quarter, columns)
    return new_base.reshape(share), new_momentum.reshape(share), keys, values


def solution(mesh):
    placed = (
        P(("replica", "fsdp"), None),
        P(),
        P(None, "fsdp", "tensor"),
        P(None, "fsdp", "tensor"),
        P("replica", None, "fsdp", "tensor"),
    )
    return jax.shard_map(
        on_device,
        mesh=mesh,
        in_specs=placed,
        out_specs=(
            P(None, ("fsdp", "replica"), "tensor"),
            P(None, ("fsdp", "replica"), "tensor"),
            P(("replica", "fsdp"), "tensor"),
            P(("replica", "fsdp"), "tensor"),
        ),
        check_vma=False,
    )
```

time: 264 us -> 120 us (0.45)
  waiting for transfers between devices: 158 us -> 0 us
  Pallas kernels: 0 us -> 113 us
  matrix products: 58.3 us -> 0 us
  other arithmetic: 31 us -> 0 us
  between operations: 14.1 us -> 0.67 us
  local copies, waits for them, and re-layouts: 0.01 us -> 6.16 us
    pallas_call x0 -> x1, Pallas kernels: none -> 113 us  [on_device(): pl.pallas_call(functools.partial(kernel, depth), name='outer_step', out_s...]
    all_gather x1 -> x0, waiting for transfers between devices: 111 us -> none  [on_device(): lax.all_gather(weights, ('replica', 'fsdp'), axis=1, tiled=True)]
    dot_general x32 -> x0, matrix products: 58.3 us -> none  [the longest x16 29.2 us: add_block(): jnp.dot(columns, portion[1], preferred_element_type=jnp.float32)]
    reduce_scatter x1 -> x0, waiting for transfers between devices: 47.4 us -> none  [on_device(): lax.psum_scatter(terms.astype(jnp.bfloat16), 'replica', scatter_dimension...]
    convert_element_type x5 -> x0, other arithmetic: 25.9 us -> none  [the longest x1 10.4 us: normalize(): return (inputs * scale * norm_gain).astype(jnp.bfloat16)]
    unnamed x2 -> x10, local copies, waits for them, and re-layouts: 0.01 us -> 6.16 us
    reduce_sum x1 -> x0, other arithmetic: 5.1 us -> none  [normalize(): jnp.mean(inputs * inputs, axis=-1, keepdims=True) + epsilon]
  transfers between devices with their start and end apart: 2 -> 0, of which waited for: 2 -> 0; matrix products, arithmetic and copies ran while one was open for 6% -> 0% of each run, Pallas kernels for 0% -> 0%
where the time goes in v1:
time: 120 us
  Pallas kernels  113 us (94%)
  local copies, waits for them, and re-layouts  6.16 us (5%)
    pallas_call x1, Pallas kernels, on_device(): pl.pallas_call(functools.partial(kernel, depth), name='outer_step', out_s...  113 us
    unnamed x10, local copies, waits for them, and re-layouts  6.16 us

profile of v1, /device:TPU:0, one launch (start us, length us, event | category | flops | bytes accessed | tf_op | source)
XLA Modules:
  0.0 119.7 jit_solution(17510726821132147781)
XLA Ops:
  0.6 112.9 %outer_step.1 = (f32[2,2,256,512]{3,2,1,0:T(8,128)}, f32[2,2,256,512]{3,2,1,0:T(8,128)}, bf16[512,512]{1,0:T(8,128)(2,1)}, bf16[512,512]{1,0:T(8,128)(2,1)}) custom-call(bf16[512,8192]{1,0:T(8,128)(2,1)} %tok_h.1, f32[1,8192]{1,0:T(1,128)} %bitcast.11, f32[2,4,2,256,512]{4,3,2,1,0:T(8,128)} %bitcast.6, f32[2,4,2,256,512]{4,3,2,1,0:T(8,128)} %bitcast.7, ...), custom_call_target="tpu_custom_call" | custom-call | tf_op jit(solution)/shard_map/outer_step/pallas_call | solution.py:306
  113.5 0.0 copy-start
  113.5 0.0 copy-start.2
  113.5 0.0 copy-start.1
  113.6 3.2 %copy.13 = f32[2,512,512]{2,1,0:T(8,128)} copy(f32[2,512,512]{2,1,0:T(8,128)} %bitcast.10) | data formatting | bytes 4194304
  116.8 0.0 copy-done
  116.8 1.3 %copy.14 = f32[2,512,512]{2,1,0:T(8,128)} copy(f32[2,512,512]{2,1,0:T(8,128)S(1)} %bitcast.9) | data formatting | bytes 4194304
  118.1 0.0 copy-done.2
  118.1 0.8 copy.15
  118.9 0.0 copy-done.1
  118.9 0.8 copy.16
Async XLA Ops:
  113.5 3.3 %copy-start = (f32[2,2,256,512]{3,2,1,0:T(8,128)S(1)}, f32[2,2,256,512]{3,2,1,0:T(8,128)}, u32[]{:S(2)}) copy-start(f32[2,2,256,512]{3,2,1,0:T(8,128)} %get-tuple-element.9) | copy-start | bytes 6291460
  113.5 4.6 %copy-start.2 = (bf16[512,512]{1,0:T(8,128)(2,1)S(1)}, bf16[512,512]{1,0:T(8,128)(2,1)}, u32[]{:S(2)}) copy-start(bf16[512,512]{1,0:T(8,128)(2,1)} %get-tuple-element.18) | copy-start | bytes 1572868
  113.5 5.4 %copy-start.1 = (bf16[512,512]{1,0:T(8,128)(2,1)S(1)}, bf16[512,512]{1,0:T(8,128)(2,1)}, u32[]{:S(2)}) copy-start(bf16[512,512]{1,0:T(8,128)(2,1)} %get-tuple-element.19) | copy-start | bytes 1572868

commit v2 on v1

--- a/solution.py
+++ b/solution.py
@@ -11,12 +11,12 @@
 outer_rate = 0.7
 epsilon = 1e-05
 MESH = pl.DeviceIdType.MESH
-CHUNKS = 4
-FIRST_Z = 3
+HALVES = 2
+WIDTH = 256
 
 
 def kernel(
-    depth, tok_h, gain_ref, base_h, mom_h, inner_h,
+    depth, chunks, tok_h, gain_ref, base_h, mom_h, inner_h,
     nb_h, nm_h, keys_ref, values_ref,
     tok, base, inner, mom, nb, w, ps, pr, ys, yr, acc,
     in_sem, tok_sem, out_sem, ps_sem, pr_sem, ys_sem, yr_sem,
@@ -31,25 +31,34 @@
     cross = (oy * 2 + c, z, x)
     right = (r, z + 1, x)
     left = (r, z - 1, x)
-    rows = w.shape[-2]
+    rows, width = w.shape[-2:]
     token_rows = tok.shape[0]
+    strips_across = chunks // (2 * HALVES)
+    first_z = 3 * chunks // 4
+
+    def part(k):
+        return k // (HALVES * strips_across), (k // strips_across) % HALVES, k % strips_across
+
+    def strip(v):
+        return pl.ds(v * width, width)
 
     def load(k):
-        m, h = k // 2, k % 2
+        m, h, v = part(k)
         return (
-            pltpu.make_async_copy(base_h.at[m, :, h], base.at[k], in_sem.at[k, 0]),
-            pltpu.make_async_copy(inner_h.at[m, :, h], inner.at[k], in_sem.at[k, 1]),
+            pltpu.make_async_copy(base_h.at[m, :, h, :, strip(v)], base.at[k], in_sem.at[k, 0]),
+            pltpu.make_async_copy(inner_h.at[m, :, h, :, strip(v)], inner.at[k], in_sem.at[k, 1]),
         )
 
     def load_momentum(k):
-        return pltpu.make_async_copy(mom_h.at[k // 2, r, k % 2], mom.at[k], in_sem.at[k, 2])
+        m, h, v = part(k)
+        return pltpu.make_async_copy(mom_h.at[m, r, h, :, strip(v)], mom.at[k], in_sem.at[k, 2])
 
     load_tokens = pltpu.make_async_copy(tok_h, tok, tok_sem)
-    for k in range(CHUNKS):
+    for k in range(chunks):
         for copy in load(k):
             copy.start()
     load_tokens.start()
-    for k in range(CHUNKS):
+    for k in range(chunks):
         load_momentum(k).start()
     acc[...] = jnp.zeros_like(acc)
 
@@ -79,8 +88,8 @@
         return pltpu.make_async_remote_copy(
             ys.at[k], yr.at[k], ys_sem.at[k], yr_sem.at[k], device_id=cross, device_id_type=MESH)
 
-    for k in range(CHUNKS + 1):
-        if k < CHUNKS:
+    for k in range(chunks + 1):
+        if k < chunks:
             for copy in load(k):
                 copy.wait()
             ps[k, 1] = delta(k, oy * 2 + oc)
@@ -124,9 +133,9 @@
                 send_left(yl, o, k).start()
 
     def multiply(cc, yl, o, k):
-        m, h = k // 2, k % 2
-        first = pl.multiple_of(((o * 4 + yl * 2 + cc) * 2 + h) * rows, rows)
-        acc[m] += jnp.dot(tok[:, pl.ds(first, rows)], w[cc, yl, o, k], preferred_element_type=jnp.float32)
+        m, h, v = part(k)
+        first = pl.multiple_of(((o * 4 + yl * 2 + cc) * HALVES + h) * rows, rows)
+        acc[m, v] += jnp.dot(tok[:, pl.ds(first, rows)], w[cc, yl, o, k], preferred_element_type=jnp.float32)
 
     def normalize(i):
         at = pl.ds(pl.multiple_of(i * 16, 16), 16)
@@ -135,16 +144,16 @@
         tok[at, :] = (value * scale * gain_ref[...]).astype(jnp.bfloat16)
 
     def out_copies(k):
-        m, h = k // 2, k % 2
+        m, h, v = part(k)
         return (
-            pltpu.make_async_copy(nb.at[k], nb_h.at[m, h], out_sem.at[k, 0]),
-            pltpu.make_async_copy(mom.at[k], nm_h.at[m, h], out_sem.at[k, 1]),
+            pltpu.make_async_copy(nb.at[k], nb_h.at[m, h, :, strip(v)], out_sem.at[k, 0]),
+            pltpu.make_async_copy(mom.at[k], nm_h.at[m, h, :, strip(v)], out_sem.at[k, 1]),
         )
 
     load_tokens.wait()
     strips = token_rows // 16
-    for k in range(CHUNKS):
-        lax.fori_loop(k * strips // CHUNKS, (k + 1) * strips // CHUNKS, lambda i, s: (normalize(i), s)[1], 0)
+    for k in range(chunks):
+        lax.fori_loop(k * strips // chunks, (k + 1) * strips // chunks, lambda i, s: (normalize(i), s)[1], 0)
         load_momentum(k).wait()
         to_cross(k).wait_recv()
         total = (
@@ -195,9 +204,9 @@
             arrived(oc, y, z, k)
         multiply((c + cc) % 2, y, z, k)
 
-    loop(2 * CHUNKS, own_products)
-
-    late = CHUNKS - FIRST_Z
+    loop(2 * chunks, own_products)
+
+    late = chunks - first_z
 
     def first_stage(g):
         def one(k):
@@ -207,16 +216,16 @@
                 send_cross(y, o, k).start()
                 send_pair(y, o, k).start()
             both_sides(g, relay)
-        loop(FIRST_Z, one)
+        loop(first_z, one)
 
         @pl.when(g == min(2, depth - 1))
         def _():
-            for k in range(FIRST_Z, CHUNKS):
+            for k in range(first_z, chunks):
                 arrived(c, oy, z, k)
                 along(oy, z, k, True, True)
                 send_pair(oy, z, k).start()
 
-        multiply_all(g, FIRST_Z, lambda b: (y, b))
+        multiply_all(g, first_z, lambda b: (y, b))
 
     lax.fori_loop(1, depth, lambda g, s: (first_stage(g), s)[1], 0)
 
@@ -224,7 +233,7 @@
         arrived(c, oy, z, k)
         send_pair(oy, z, k).start()
 
-    loop(FIRST_Z, from_cross)
+    loop(first_z, from_cross)
 
     def cross_products(i):
         k, cc = i // 2, i % 2
@@ -234,11 +243,11 @@
             arrived(oc, oy, z, k)
         multiply((c + cc) % 2, oy, z, k)
 
-    loop(2 * CHUNKS, cross_products)
+    loop(2 * chunks, cross_products)
 
     def second_stage(g):
         def one(i):
-            yl, k = i % 2, FIRST_Z + i // 2
+            yl, k = i % 2, first_z + i // 2
 
             def relay(o, do_right, do_left):
                 arrived(c, yl, o, k)
@@ -246,38 +255,39 @@
                 send_pair(yl, o, k).start()
             both_sides(g, relay)
         loop(2 * late, one)
-        multiply_all(g, 2 * late, lambda b: (b % 2, FIRST_Z + b // 2))
+        multiply_all(g, 2 * late, lambda b: (b % 2, first_z + b // 2))
 
         def two(k):
             def relay(o, do_right, do_left):
                 arrived(c, oy, o, k)
                 send_pair(oy, o, k).start()
             both_sides(g, relay)
-        loop(FIRST_Z, two)
-        multiply_all(g, FIRST_Z, lambda b: (oy, b))
+        loop(first_z, two)
+        multiply_all(g, first_z, lambda b: (oy, b))
 
     lax.fori_loop(1, depth, lambda g, s: (second_stage(g), s)[1], 0)
 
-    keys_ref[...] = acc[0].astype(keys_ref.dtype)
-    values_ref[...] = acc[1].astype(values_ref.dtype)
-
-    for k in range(CHUNKS):
+    for v in range(strips_across):
+        keys_ref[:, strip(v)] = acc[0, v].astype(keys_ref.dtype)
+        values_ref[:, strip(v)] = acc[1, v].astype(values_ref.dtype)
+
+    for k in range(chunks):
         to_pair(k).wait_send()
         to_cross(k).wait_send()
         for copy in out_copies(k):
             copy.wait()
 
     def drain(i):
-        o, k = i // CHUNKS, i % CHUNKS
-
-        @pl.when((k < FIRST_Z) | (o == z))
+        o, k = i // chunks, i % chunks
+
+        @pl.when((k < first_z) | (o == z))
         def _():
             send_cross(y, o, k).wait_send()
 
         for yl in range(2):
             send_pair(yl, o, k).wait_send()
 
-            @pl.when((k >= FIRST_Z) | (yl == y))
+            @pl.when((k >= first_z) | (yl == y))
             def _():
                 @pl.when((o <= z) & (z < depth - 1))
                 def _():
@@ -287,7 +297,7 @@
                 def _():
                     send_left(yl, o, k).wait_send()
 
-    loop(depth * CHUNKS, drain)
+    loop(depth * chunks, drain)
 
 
 def on_device(tokens, norm_gain, outer_base, momentum, inner_params):
@@ -295,20 +305,22 @@
     replicas = lax.axis_size("replica")
     assert replicas == 4
     quarter = outer_base.shape[1] // replicas
-    rows, columns = quarter // 2, outer_base.shape[2]
+    rows, columns = quarter // HALVES, outer_base.shape[2]
+    width = WIDTH if columns % WIDTH == 0 else columns
+    chunks = 2 * HALVES * (columns // width)
     count, features = tokens.shape
-    split = (2, replicas, 2, rows, columns)
+    split = (2, replicas, HALVES, rows, columns)
     anywhere = pl.BlockSpec(memory_space=pl.ANY)
     vmem = pl.BlockSpec(memory_space=pltpu.VMEM)
     dma = pltpu.SemaphoreType.DMA
     f32, bf16 = jnp.float32, jnp.bfloat16
-    piece = (rows, columns)
+    piece, half = (rows, width), (rows, columns)
     new_base, new_momentum, keys, values = pl.pallas_call(
-        functools.partial(kernel, depth),
+        functools.partial(kernel, depth, chunks),
         name="outer_step",
         out_shape=(
-            jax.ShapeDtypeStruct((2, 2) + piece, f32),
-            jax.ShapeDtypeStruct((2, 2) + piece, f32),
+            jax.ShapeDtypeStruct((2, HALVES) + half, f32),
+            jax.ShapeDtypeStruct((2, HALVES) + half, f32),
             jax.ShapeDtypeStruct((count, columns), bf16),
             jax.ShapeDtypeStruct((count, columns), bf16),
         ),
@@ -316,20 +328,20 @@
         out_specs=(anywhere, anywhere, vmem, vmem),
         scratch_shapes=[
             pltpu.VMEM((count, features), bf16),
-            pltpu.VMEM((CHUNKS, replicas) + piece, f32),
-            pltpu.VMEM((CHUNKS, replicas) + piece, bf16),
-            pltpu.VMEM((CHUNKS,) + piece, f32),
-            pltpu.VMEM((CHUNKS,) + piece, f32),
-            pltpu.VMEM((2, 2, depth, CHUNKS) + piece, bf16),
-            pltpu.VMEM((CHUNKS, 2) + piece, bf16),
-            pltpu.VMEM((CHUNKS, 2) + piece, bf16),
-            pltpu.VMEM((CHUNKS,) + piece, bf16),
-            pltpu.VMEM((CHUNKS,) + piece, bf16),
-            pltpu.VMEM((2, count, columns), f32),
-            dma((CHUNKS, 3)), dma, dma((CHUNKS, 2)),
-            dma((CHUNKS,)), dma((CHUNKS,)), dma((CHUNKS,)), dma((CHUNKS,)),
-            dma((2, 2, depth, CHUNKS)),
-            dma((2, depth, CHUNKS)), dma((2, depth, CHUNKS)), dma((depth, CHUNKS)), dma((2, depth, CHUNKS)),
+            pltpu.VMEM((chunks, replicas) + piece, f32),
+            pltpu.VMEM((chunks, replicas) + piece, bf16),
+            pltpu.VMEM((chunks,) + piece, f32),
+            pltpu.VMEM((chunks,) + piece, f32),
+            pltpu.VMEM((2, 2, depth, chunks) + piece, bf16),
+            pltpu.VMEM((chunks, 2) + piece, bf16),
+            pltpu.VMEM((chunks, 2) + piece, bf16),
+            pltpu.VMEM((chunks,) + piece, bf16),
+            pltpu.VMEM((chunks,) + piece, bf16),
+            pltpu.VMEM((2, columns // width, count, width), f32),
+            dma((chunks, 3)), dma, dma((chunks, 2)),
+            dma((chunks,)), dma((chunks,)), dma((chunks,)), dma((chunks,)),
+            dma((2, 2, depth, chunks)),
+            dma((2, depth, chunks)), dma((2, depth, chunks)), dma((depth, chunks)), dma((2, depth, chunks)),
         ],
         compiler_params=pltpu.CompilerParams(
             collective_id=0, has_side_effects=True, vmem_limit_bytes=60 * 1024 * 1024),

time: 120 us -> 126 us (1.050)
  Pallas kernels: 113 us -> 119 us
    pallas_call x1, Pallas kernels: 113 us -> 119 us  [on_device(): pl.pallas_call(functools.partial(kernel, depth, chunks), name='outer_step...]
where the time goes in v2:
time: 126 us
  Pallas kernels  119 us (94%)
  local copies, waits for them, and re-layouts  6.16 us (5%)
    pallas_call x1, Pallas kernels, on_device(): pl.pallas_call(functools.partial(kernel, depth, chunks), name='outer_step...  119 us
    unnamed x10, local copies, waits for them, and re-layouts  6.16 us

profile of v2, /device:TPU:0, one launch (start us, length us, event | category | flops | bytes accessed | tf_op | source)
XLA Modules:
  0.0 125.5 jit_solution(1303984227138914489)
XLA Ops:
  0.6 118.7 %outer_step.1 = (f32[2,2,256,512]{3,2,1,0:T(8,128)}, f32[2,2,256,512]{3,2,1,0:T(8,128)}, bf16[512,512]{1,0:T(8,128)(2,1)}, bf16[512,512]{1,0:T(8,128)(2,1)}) custom-call(bf16[512,8192]{1,0:T(8,128)(2,1)} %tok_h.1, f32[1,8192]{1,0:T(1,128)} %bitcast.11, f32[2,4,2,256,512]{4,3,2,1,0:T(8,128)} %bitcast.6, f32[2,4,2,256,512]{4,3,2,1,0:T(8,128)} %bitcast.7, ...), custom_call_target="tpu_custom_call" | custom-call | tf_op jit(solution)/shard_map/outer_step/pallas_call | solution.py:318
  119.3 0.0 copy-start
  119.3 0.0 copy-start.2
  119.4 0.0 copy-start.1
  119.4 3.2 %copy.13 = f32[2,512,512]{2,1,0:T(8,128)} copy(f32[2,512,512]{2,1,0:T(8,128)} %bitcast.10) | data formatting | bytes 4194304
  122.6 0.0 copy-done
  122.6 1.3 %copy.14 = f32[2,512,512]{2,1,0:T(8,128)} copy(f32[2,512,512]{2,1,0:T(8,128)S(1)} %bitcast.9) | data formatting | bytes 4194304
  123.9 0.0 copy-done.2
  123.9 0.8 copy.15
  124.7 0.0 copy-done.1
  124.7 0.8 copy.16
Async XLA Ops:
  119.3 3.3 %copy-start = (f32[2,2,256,512]{3,2,1,0:T(8,128)S(1)}, f32[2,2,256,512]{3,2,1,0:T(8,128)}, u32[]{:S(2)}) copy-start(f32[2,2,256,512]{3,2,1,0:T(8,128)} %get-tuple-element.9) | copy-start | bytes 6291460
  119.3 4.6 %copy-start.2 = (bf16[512,512]{1,0:T(8,128)(2,1)S(1)}, bf16[512,512]{1,0:T(8,128)(2,1)}, u32[]{:S(2)}) copy-start(bf16[512,512]{1,0:T(8,128)(2,1)} %get-tuple-element.18) | copy-start | bytes 1572868
  119.4 5.4 %copy-start.1 = (bf16[512,512]{1,0:T(8,128)(2,1)S(1)}, bf16[512,512]{1,0:T(8,128)(2,1)}, u32[]{:S(2)}) copy-start(bf16[512,512]{1,0:T(8,128)(2,1)} %get-tuple-element.19) | copy-start | bytes 1572868

commit v3 on v1

--- a/solution.py
+++ b/solution.py
@@ -248,13 +248,26 @@
         loop(2 * late, one)
         multiply_all(g, 2 * late, lambda b: (b % 2, FIRST_Z + b // 2))
 
+        def product(cc, k):
+            def one_side(o, *_):
+                @pl.when(cc == oc)
+                def _():
+                    arrived(oc, oy, o, k)
+                multiply(cc, oy, o, k)
+            both_sides(g, one_side)
+
         def two(k):
             def relay(o, do_right, do_left):
                 arrived(c, oy, o, k)
                 send_pair(oy, o, k).start()
             both_sides(g, relay)
+            product(c, k)
+
+            @pl.when(k > 0)
+            def _():
+                product(oc, k - 1)
         loop(FIRST_Z, two)
-        multiply_all(g, FIRST_Z, lambda b: (oy, b))
+        product(oc, FIRST_Z - 1)
 
     lax.fori_loop(1, depth, lambda g, s: (second_stage(g), s)[1], 0)
 

time: 120 us -> 118 us (0.983)
  Pallas kernels: 113 us -> 111 us
    pallas_call x1, Pallas kernels: 113 us -> 111 us  [on_device(): pl.pallas_call(functools.partial(kernel, depth), name='outer_step', out_s...]
where the time goes in v3:
time: 118 us
  Pallas kernels  111 us (94%)
  local copies, waits for them, and re-layouts  6.16 us (5%)
    pallas_call x1, Pallas kernels, on_device(): pl.pallas_call(functools.partial(kernel, depth), name='outer_step', out_s...  111 us
    unnamed x10, local copies, waits for them, and re-layouts  6.16 us

profile of v3, /device:TPU:0, one launch (start us, length us, event | category | flops | bytes accessed | tf_op | source)
XLA Modules:
  0.0 117.7 jit_solution(16441952865573557955)
XLA Ops:
  0.6 110.8 %outer_step.1 = (f32[2,2,256,512]{3,2,1,0:T(8,128)}, f32[2,2,256,512]{3,2,1,0:T(8,128)}, bf16[512,512]{1,0:T(8,128)(2,1)}, bf16[512,512]{1,0:T(8,128)(2,1)}) custom-call(bf16[512,8192]{1,0:T(8,128)(2,1)} %tok_h.1, f32[1,8192]{1,0:T(1,128)} %bitcast.11, f32[2,4,2,256,512]{4,3,2,1,0:T(8,128)} %bitcast.6, f32[2,4,2,256,512]{4,3,2,1,0:T(8,128)} %bitcast.7, ...), custom_call_target="tpu_custom_call" | custom-call | tf_op jit(solution)/shard_map/outer_step/pallas_call | solution.py:319
  111.5 0.0 copy-start
  111.5 0.0 copy-start.2
  111.5 0.0 copy-start.1
  111.5 3.2 %copy.13 = f32[2,512,512]{2,1,0:T(8,128)} copy(f32[2,512,512]{2,1,0:T(8,128)} %bitcast.10) | data formatting | bytes 4194304
  114.7 0.0 copy-done
  114.7 1.3 %copy.14 = f32[2,512,512]{2,1,0:T(8,128)} copy(f32[2,512,512]{2,1,0:T(8,128)S(1)} %bitcast.9) | data formatting | bytes 4194304
  116.1 0.0 copy-done.2
  116.1 0.8 copy.15
  116.9 0.0 copy-done.1
  116.9 0.8 copy.16
Async XLA Ops:
  111.5 3.3 %copy-start = (f32[2,2,256,512]{3,2,1,0:T(8,128)S(1)}, f32[2,2,256,512]{3,2,1,0:T(8,128)}, u32[]{:S(2)}) copy-start(f32[2,2,256,512]{3,2,1,0:T(8,128)} %get-tuple-element.9) | copy-start | bytes 6291460
  111.5 4.6 %copy-start.2 = (bf16[512,512]{1,0:T(8,128)(2,1)S(1)}, bf16[512,512]{1,0:T(8,128)(2,1)}, u32[]{:S(2)}) copy-start(bf16[512,512]{1,0:T(8,128)(2,1)} %get-tuple-element.18) | copy-start | bytes 1572868
  111.5 5.4 %copy-start.1 = (bf16[512,512]{1,0:T(8,128)(2,1)S(1)}, bf16[512,512]{1,0:T(8,128)(2,1)}, u32[]{:S(2)}) copy-start(bf16[512,512]{1,0:T(8,128)(2,1)} %get-tuple-element.19) | copy-start | bytes 1572868
